TPU v7x, 256 devices: a whole 4x4x8 slice. The times are simulated.
256 devices in a mesh: dp: 32 (over z, y), block: 8 (over x, core).
Axes of the slice: x: 4, y: 4, z: 8, core: 2. Of those that a mesh axis runs over, the one named last changes fastest.
Arguments:
- x_act: bfloat16 [8, 16384, 4096], P('block', 'dp')
- g_out: bfloat16 [8, 16384, 4096], P('block', 'dp')
- proj_in: bfloat16 [8, 4096, 64], P('block'), may hold values from -0.09375 to 0.09375
- proj_out: bfloat16 [8, 4096, 64], P('block'), may hold values from -0.09375 to 0.09375
- queries: bfloat16 [8, 2048, 4096], P('block', 'dp'), may hold values from -6 to 6
- cand_ids: int32 [32, 32, 2], P('dp'), may hold values from 0 to 15, as said below
- cand_counts: int32 [32, 32], P('dp'), may hold values from 0 to 2, as said below
Outputs:
- scores: float32 [2048, 128], P(('dp', 'block'))
Inputs may be any that keep to these rules, and one draw needn't show every extreme that they name: `cand_ids`: each list of a training shard d for an owner p names 2 distinct query blocks of p; slots at or past cand_counts[d, p] are padding. Every training shard d has cand_counts[d, d] = 2.
All inputs are finite; a program needn't handle non-finite values.
Results may differ from a plain program's by a relative error of at most 0.0096.
Values may be sent and summed in bfloat16 or wider, within the bound.
No kernel may reach another device: no remote copies, remote signals or barrier semaphores. Data moves between devices by JAX's collectives and lax.ppermute only.
A program may use at most 64 MiB of HBM per device.

v0:
```python
import jax
import jax.numpy as jnp
from jax import lax
from jax.sharding import PartitionSpec as P

E_DEV = 4
SEQ = 128
QB = 4
CAP = 2
DAMP = 0.1


def kron_inverse(factor):
    width = factor.shape[0]
    identity = jnp.eye(width, dtype=jnp.float32)
    damping = DAMP * jnp.trace(factor) / width + 1e-06
    lower_factor = jnp.linalg.cholesky(factor + damping * identity)
    return jax.scipy.linalg.cho_solve((lower_factor, True), identity)


def body(x_act, g_out, proj_in, proj_out, queries, cand_ids, cand_counts):
    act_rows = x_act[0]
    grad_rows = g_out[0]
    row_count = act_rows.shape[0]
    width = proj_in.shape[2]
    n_owners = lax.axis_size("dp")
    n_layers = lax.axis_size("block")
    act_proj = jnp.dot(act_rows, proj_in[0], preferred_element_type=jnp.float32).astype(
        jnp.bfloat16
    )
    grad_proj = jnp.dot(grad_rows, proj_out[0], preferred_element_type=jnp.float32).astype(
        jnp.bfloat16
    )
    contract_rows = (((0,), (0,)), ((), ()))
    part_a = lax.dot_general(act_proj, act_proj, contract_rows, preferred_element_type=jnp.float32)
    part_g = lax.dot_general(
        grad_proj, grad_proj, contract_rows, preferred_element_type=jnp.float32
    )
    factor_a, factor_g = lax.psum((part_a, part_g), "dp")
    token_total = row_count * n_owners
    inverse_a = kron_inverse(factor_a / token_total)
    inverse_g = kron_inverse(factor_g / token_total)
    act_three = act_proj.reshape(E_DEV, SEQ, width)
    grad_three = grad_proj.reshape(E_DEV, SEQ, width)
    example_grad = (
        jnp.einsum("esi,esj->eij", grad_three, act_three, preferred_element_type=jnp.float32) / SEQ
    )
    left_side = jnp.einsum("ij,ejk->eik", inverse_g, example_grad, precision=lax.Precision.HIGHEST)
    precond = jnp.einsum("eik,kl->eil", left_side, inverse_a, precision=lax.Precision.HIGHEST)
    precond = precond.reshape(E_DEV, width * width).astype(jnp.bfloat16)
    req_ids, req_counts = (
        lax.all_to_all(cand_ids, "dp", split_axis=1, concat_axis=0, tiled=True),
        lax.all_to_all(cand_counts, "dp", split_axis=1, concat_axis=0, tiled=True),
    )
    req_ids = req_ids.reshape(n_owners, CAP)
    req_counts = req_counts.reshape(n_owners)
    query_rows = queries[0]
    owned = query_rows.shape[0]
    block_count = owned // QB
    slot_live = jnp.arange(CAP)[None, :] < req_counts[:, None]
    onehot = (
        (req_ids[:, :, None] == jnp.arange(block_count)[None, None, :]) & slot_live[:, :, None]
    ).astype(jnp.float32)
    dense_part = lax.dot_general(
        query_rows,
        lax.all_gather(precond, "dp", axis=0, tiled=True),
        (((1,), (1,)), ((), ())),
        preferred_element_type=jnp.float32,
    )
    live_blocks = jnp.sum(onehot, axis=1)
    mask_full = jnp.broadcast_to(
        jnp.transpose(live_blocks)[:, None, :, None], (block_count, QB, n_owners, E_DEV)
    ).reshape(owned, n_owners * E_DEV)
    layer_part = dense_part * mask_full
    scale = 1.0 / float(width * width * n_layers) ** 0.5
    return lax.psum_scatter(layer_part * scale, "block", scatter_dimension=0, tiled=True)


def solution(mesh):
    return jax.shard_map(
        body,
        mesh=mesh,
        in_specs=(
            P("block", "dp", None),
            P("block", "dp", None),
            P("block", None, None),
            P("block", None, None),
            P("block", "dp", None),
            P("dp", None, None),
            P("dp", None),
        ),
        out_specs=P(("dp", "block"), None),
        check_vma=False,
    )
```

profile of v0, /device:TPU:64, one launch (start us, length us, event | category | flops | bytes accessed | tf_op | source)
XLA Modules:
  0.0 291.4 jit_solution(2975817334751202043)
XLA Ops:
  6.5 1.0 copy-done
  7.6 3.7 %fusion.4 = bf16[512,64]{0,1:T(8,128)(2,1)S(1)} fusion(bf16[1,512,4096]{2,1,0:T(8,128)(2,1)} %param.11, bf16[1,4096,64]{1,2,0:T(8,128)(2,1)S(1)} %copy-done), kind=kOutput, calls=%fused_computation.6 | convolution fusion | flops 268468224 | bytes 4784128 | tf_op jit(solution)/shard_map/dot_general | solution.py:31
  11.5 1.4 fusion.7
  13.2 133.0 %all-reduce.1 = (f32[64,64]{0,1:T(8,128)S(1)}, f32[64,64]{0,1:T(8,128)S(1)}) all-reduce(f32[64,64]{0,1:T(8,128)S(1)} %fusion.32, f32[64,64]{0,1:T(8,128)S(1)} %fusion.33), channel_id=1, replica_groups=mesh['dp'=32,'block'=8] {'dp'}, use_global_device_ids=true, to_apply=%region_0.0 | all-reduce | flops 8192 | bytes 65536 | tf_op jit(solution)/shard_map/psum | solution.py:39
  146.2 0.7 select_reduce_fusion.3
  149.0 5.8 %cholesky.55 = f32[64,64]{1,0:T(8,128)S(1)} custom-call(f32[64,64]{1,0:T(8,128)S(1)} %fusion.27), custom_call_target="Cholesky" | custom-call | tf_op jit(solution)/shard_map/jit(cholesky)/cholesky | solution.py:17
  154.9 0.6 compare_reduce_fusion
  155.5 0.7 fusion.24
  156.2 4.9 %custom-call.9 = f32[1,64,64]{1,2,0:T(8,128)S(1)} custom-call(f32[1,64,64]{2,1,0:T(8,128)S(1)} %fusion.24), custom_call_target="InvertDiagBlocksLowerTriangular" | custom-call | tf_op jit(solution)/shard_map/jit(_cho_solve)/triangular_solve | solution.py:18
  161.6 5.8 %cholesky.44 = f32[64,64]{1,0:T(8,128)S(1)} custom-call(f32[64,64]{1,0:T(8,128)S(1)} %fusion.30), custom_call_target="Cholesky" | custom-call | tf_op jit(solution)/shard_map/jit(cholesky)/cholesky | solution.py:17
  168.1 0.7 fusion.23
  168.8 4.9 %custom-call.8 = f32[1,64,64]{1,2,0:T(8,128)S(1)} custom-call(f32[1,64,64]{2,1,0:T(8,128)S(1)} %fusion.23), custom_call_target="InvertDiagBlocksLowerTriangular" | custom-call | tf_op jit(solution)/shard_map/jit(_cho_solve)/triangular_solve | solution.py:18
  174.9 0.7 reshape.60
  175.6 0.7 copy.52
  176.3 16.2 %all-to-all-start.1 = ((s32[1,32,1]{2,0,1:T(1,128)}), s32[1,32,1]{2,0,1:T(1,128)S(1)}, u32[]{:S(2)}, u32[]{:S(2)}) async-start(s32[1,32,1]{2,0,1:T(1,128)} %copy.52), calls=%async_computation.1 | async-start | bytes 32768 | tf_op jit(solution)/shard_map/all_to_all | solution.py:53
  192.5 0.7 copy.50
  194.4 5.8 %all-to-all-done.1 = s32[1,32,1]{2,0,1:T(1,128)S(1)} async-done(((s32[1,32,1]{2,0,1:T(1,128)}), s32[1,32,1]{2,0,1:T(1,128)S(1)}, u32[]{:S(2)}, u32[]{:S(2)}) %all-to-all-start.1) | async-done | bytes 160 | tf_op jit(solution)/shard_map/all_to_all | solution.py:53
  200.3 5.6 %all-to-all-start = ((s32[1,32,2]{2,0,1:T(1,128)}), s32[1,32,2]{2,0,1:T(1,128)S(1)}, u32[]{:S(2)}, u32[]{:S(2)}) async-start(s32[1,32,2]{2,0,1:T(1,128)} %copy.50), calls=%async_computation | async-start | bytes 32768 | tf_op jit(solution)/shard_map/all_to_all | solution.py:52
  205.9 0.7 reduce.4
  206.5 7.1 %all-to-all-done = s32[1,32,2]{2,0,1:T(1,128)S(1)} async-done(((s32[1,32,2]{2,0,1:T(1,128)}), s32[1,32,2]{2,0,1:T(1,128)S(1)}, u32[]{:S(2)}, u32[]{:S(2)}) %all-to-all-start) | async-done | bytes 288 | tf_op jit(solution)/shard_map/all_to_all | solution.py:52
  213.9 0.6 reshape.59
  214.6 43.9 %all-gather.3.cloned.1.call-done = bf16[32,4,4096]{2,1,0:T(4,128)(2,1)} async-done(((bf16[1,4,4096]{2,1,0:T(4,128)(2,1)}), bf16[32,4,4096]{2,1,0:T(4,128)(2,1)}) %all-gather.3.cloned.1.call-update) | async-done | bytes 1048592 | tf_op jit(solution)/shard_map/all_gather | solution.py:66
  258.5 1.3 reshape.61
  260.4 23.6 %all-reduce = f32[64,128]{1,0:T(8,128)S(1)} all-reduce(f32[64,128]{1,0:T(8,128)S(1)} %fusion.11), channel_id=2, replica_groups=mesh['dp'=32,'block'=8] {'block'}, use_global_device_ids=true, to_apply=%region_7.10.clone | all-reduce | flops 8192 | bytes 65536
  (40 shorter events, 5.5 us)
Async XLA Ops:
  6.5 1.0 copy-start
  6.5 5.0 %copy-start.2 = (bf16[1,4096,64]{1,2,0:T(8,128)(2,1)S(1)}, bf16[1,4096,64]{1,2,0:T(8,128)(2,1)}, u32[]{:S(2)}) copy-start(bf16[1,4096,64]{1,2,0:T(8,128)(2,1)} %param.12) | copy-start | bytes 1572868
  6.5 252.0 %all-gather.3.cloned.1.call-start = ((), (), s32[]{:S(2)}) async-start(), calls=%async_computation.2 | async-start | bytes 1081344 | tf_op jit(solution)/shard_map/all_gather | solution.py:66
  7.6 3.9 %copy-start.1 = (bf16[1,512,4096]{2,1,0:T(8,128)(2,1)S(1)}, bf16[1,512,4096]{2,1,0:T(8,128)(2,1)}, u32[]{:S(2)}) copy-start(bf16[1,512,4096]{2,1,0:T(8,128)(2,1)} %param.10) | copy-start | bytes 12582916
  11.3 164.3 %copy-start.5 = (s32[1,32]{1,0:T(1,128)S(1)}, s32[1,32]{1,0:T(1,128)}, u32[]{:S(2)}) copy-start(s32[1,32]{1,0:T(1,128)} %param.16) | copy-start | bytes 388
  11.3 181.2 %copy-start.4 = (s32[1,32,2]{1,2,0:T(2,128)S(1)}, s32[1,32,2]{1,2,0:T(2,128)}, u32[]{:S(2)}) copy-start(s32[1,32,2]{1,2,0:T(2,128)} %param.15) | copy-start | bytes 772
  11.3 181.9 %copy-start.6 = (u32[256]{0:T(256)S(1)}, u32[256]{0:T(256)}, u32[]{:S(2)}) copy-start(u32[256]{0:T(256)} %constant.72) | copy-start | bytes 3076
  12.9 247.0 %copy-start.3 = (bf16[1,64,4096]{2,1,0:T(8,128)(2,1)S(1)}, bf16[1,64,4096]{2,1,0:T(8,128)(2,1)}, u32[]{:S(2)}) copy-start(bf16[1,64,4096]{2,1,0:T(8,128)(2,1)} %param.14) | copy-start | bytes 1572868
  176.3 24.0 %all-to-all-start.1 = ((s32[1,32,1]{2,0,1:T(1,128)}), s32[1,32,1]{2,0,1:T(1,128)S(1)}, u32[]{:S(2)}, u32[]{:S(2)}) async-start(s32[1,32,1]{2,0,1:T(1,128)} %copy.52), calls=%async_computation.1 | async-start | bytes 32768 | tf_op jit(solution)/shard_map/all_to_all | solution.py:53
  200.3 13.4 %all-to-all-start = ((s32[1,32,2]{2,0,1:T(1,128)}), s32[1,32,2]{2,0,1:T(1,128)S(1)}, u32[]{:S(2)}, u32[]{:S(2)}) async-start(s32[1,32,2]{2,0,1:T(1,128)} %copy.50), calls=%async_computation | async-start | bytes 32768 | tf_op jit(solution)/shard_map/all_to_all | solution.py:52
Sparse Core Ops, SparseCore 0:
  175.7 82.7 all-gather.2
where the time goes:
time: 292 us; the launch traced here: 291 us
  blocking collectives  157 us (54%)
  waiting for transfers between devices  56.9 us (19%)
  other arithmetic  26.1 us (9%)
  starting transfers between devices  21.8 us (7%)
  between operations  15.6 us (5%)
  matrix products  7.64 us (3%)
  local copies, waits for them, and re-layouts  6.72 us (2%)
    psum x1, blocking collectives, body(): factor_a, factor_g = lax.psum((part_a, part_g), 'dp')  133 us
    all_gather x1, waiting for transfers between devices, body(): lax.all_gather(precond, 'dp', axis=0, tiled=True)  43.9 us
    unnamed x1, blocking collectives  23.6 us
    all_to_all x1, starting transfers between devices, body(): lax.all_to_all(cand_counts, 'dp', split_axis=1, concat_axis=0, tiled=True)  16.2 us
    another operation x6, other arithmetic, kron_inverse(): lower_factor = jnp.linalg.cholesky(factor + damping * identity)  13 us
    another operation x4, other arithmetic, kron_inverse(): return jax.scipy.linalg.cho_solve((lower_factor, True), identity)  11.1 us
    all_to_all x1, waiting for transfers between devices, body(): lax.all_to_all(cand_ids, 'dp', split_axis=1, concat_axis=0, tiled=True)  7.09 us
  transfers between devices with their start and end apart: 3, of which 3 were waited for; matrix products, arithmetic and copies ran while one was open for 1% of the time, Pallas kernels for 0%

commit v1 on v0

--- a/solution.py
+++ b/solution.py
@@ -19,6 +19,12 @@
 
 
 def body(x_act, g_out, proj_in, proj_out, queries, cand_ids, cand_counts):
+
+    def _resolve_sample(content):
+        return jnp.concatenate(
+            lax.all_to_all(jnp.stack(lax.axis_size("dp") * [content], 0), "dp", 0, 0), 0
+        )
+
     act_rows = x_act[0]
     grad_rows = g_out[0]
     row_count = act_rows.shape[0]
@@ -63,7 +69,7 @@
     ).astype(jnp.float32)
     dense_part = lax.dot_general(
         query_rows,
-        lax.all_gather(precond, "dp", axis=0, tiled=True),
+        _resolve_sample(precond),
         (((1,), (1,)), ((), ())),
         preferred_element_type=jnp.float32,
     )

time: 292 us -> 254 us (0.87)
  waiting for transfers between devices: 56.9 us -> 22.7 us
  between operations: 15.6 us -> 2.13 us
  starting transfers between devices: 21.8 us -> 34.1 us
  blocking collectives: 157 us -> 154 us
    all_gather x1 -> x0, waiting for transfers between devices: 43.9 us -> none  [body(): lax.all_gather(precond, 'dp', axis=0, tiled=True)]
    all_to_all x0 -> x1, waiting for transfers between devices: none -> 15.5 us  [_resolve_sample(): lax.all_to_all(jnp.stack(lax.axis_size('dp') * [content], 0), 'dp', 0, 0)]
    all_to_all x1, starting transfers between devices: 5.59 us -> 17.3 us  [body(): lax.all_to_all(cand_ids, 'dp', split_axis=1, concat_axis=0, tiled=True)]
    all_to_all x0 -> x1, starting transfers between devices: none -> 5.91 us  [_resolve_sample(): lax.all_to_all(jnp.stack(lax.axis_size('dp') * [content], 0), 'dp', 0, 0)]
    all_to_all x1, waiting for transfers between devices: 5.84 us -> 0.01 us  [body(): lax.all_to_all(cand_counts, 'dp', split_axis=1, concat_axis=0, tiled=True)]
    all_to_all x1, starting transfers between devices: 16.2 us -> 10.9 us  [body(): lax.all_to_all(cand_counts, 'dp', split_axis=1, concat_axis=0, tiled=True)]
    unnamed x19 -> x15, local copies, waits for them, and re-layouts: 4.98 us -> 1.9 us
  transfers between devices with their start and end apart: 3 -> 3, of which waited for: 3 -> 2; matrix products, arithmetic and copies ran while one was open for 1% -> 14% of each run, Pallas kernels for 0% -> 0%
where the time goes in v1:
time: 254 us; the launch traced here: 253 us
  blocking collectives  154 us (61%)
  starting transfers between devices  34.1 us (13%)
  other arithmetic  26.1 us (10%)
  waiting for transfers between devices  22.7 us (9%)
  matrix products  7.65 us (3%)
  local copies, waits for them, and re-layouts  6.21 us (2%)
    psum x1, blocking collectives, body(): factor_a, factor_g = lax.psum((part_a, part_g), 'dp')  130 us
    unnamed x1, blocking collectives  23.6 us
    all_to_all x1, starting transfers between devices, body(): lax.all_to_all(cand_ids, 'dp', split_axis=1, concat_axis=0, tiled=True)  17.3 us
    all_to_all x1, waiting for transfers between devices, _resolve_sample(): lax.all_to_all(jnp.stack(lax.axis_size('dp') * [content], 0), 'dp', 0, 0)  15.5 us
    another operation x6, other arithmetic, kron_inverse(): lower_factor = jnp.linalg.cholesky(factor + damping * identity)  13 us
    another operation x4, other arithmetic, kron_inverse(): return jax.scipy.linalg.cho_solve((lower_factor, True), identity)  11.1 us
    all_to_all x1, starting transfers between devices, body(): lax.all_to_all(cand_counts, 'dp', split_axis=1, concat_axis=0, tiled=True)  10.9 us
    all_to_all x1, waiting for transfers between devices, body(): lax.all_to_all(cand_ids, 'dp', split_axis=1, concat_axis=0, tiled=True)  7.19 us
  transfers between devices with their start and end apart: 3, of which 2 were waited for; matrix products, arithmetic and copies ran while one was open for 14% of the time, Pallas kernels for 0%

profile of v1, /device:TPU:64, one launch (start us, length us, event | category | flops | bytes accessed | tf_op | source)
XLA Modules:
  0.0 253.0 jit_solution(6339354013856781801)
XLA Ops:
  0.0 1.4 copy.52
  1.4 10.9 %all-to-all-start.2 = ((s32[1,32,1]{2,0,1:T(1,128)}), s32[1,32,1]{2,0,1:T(1,128)S(1)}, u32[]{:S(2)}, u32[]{:S(2)}) async-start(s32[1,32,1]{2,0,1:T(1,128)} %copy.52), calls=%async_computation.2 | async-start | bytes 32768 | tf_op jit(solution)/shard_map/all_to_all | solution.py:59
  12.4 3.7 %fusion.4 = bf16[512,64]{0,1:T(8,128)(2,1)S(1)} fusion(bf16[1,512,4096]{2,1,0:T(8,128)(2,1)} %param.11, bf16[1,4096,64]{1,2,0:T(8,128)(2,1)S(1)} %copy-done), kind=kOutput, calls=%fused_computation.6 | convolution fusion | flops 268468224 | bytes 4784128 | tf_op jit(solution)/shard_map/dot_general | solution.py:37
  16.3 1.4 fusion.7
  18.0 130.5 %all-reduce.1 = (f32[64,64]{0,1:T(8,128)S(1)}, f32[64,64]{0,1:T(8,128)S(1)}) all-reduce(f32[64,64]{0,1:T(8,128)S(1)} %fusion.32, f32[64,64]{0,1:T(8,128)S(1)} %fusion.33), channel_id=1, replica_groups=mesh['dp'=32,'block'=8] {'dp'}, use_global_device_ids=true, to_apply=%region_0.0 | all-reduce | flops 8192 | bytes 65536 | tf_op jit(solution)/shard_map/psum | solution.py:45
  148.5 0.6 select_reduce_fusion.3
  149.1 0.6 select_reduce_fusion.2
  151.0 5.8 %cholesky.55 = f32[64,64]{1,0:T(8,128)S(1)} custom-call(f32[64,64]{1,0:T(8,128)S(1)} %fusion.27), custom_call_target="Cholesky" | custom-call | tf_op jit(solution)/shard_map/jit(cholesky)/cholesky | solution.py:17
  156.9 0.6 compare_reduce_fusion
  157.5 0.7 fusion.24
  158.2 4.9 %custom-call.9 = f32[1,64,64]{1,2,0:T(8,128)S(1)} custom-call(f32[1,64,64]{2,1,0:T(8,128)S(1)} %fusion.24), custom_call_target="InvertDiagBlocksLowerTriangular" | custom-call | tf_op jit(solution)/shard_map/jit(_cho_solve)/triangular_solve | solution.py:18
  163.4 5.8 %cholesky.44 = f32[64,64]{1,0:T(8,128)S(1)} custom-call(f32[64,64]{1,0:T(8,128)S(1)} %fusion.30), custom_call_target="Cholesky" | custom-call | tf_op jit(solution)/shard_map/jit(cholesky)/cholesky | solution.py:17
  169.3 0.6 compare_reduce_fusion.1
  170.0 0.7 fusion.23
  170.6 4.9 %custom-call.8 = f32[1,64,64]{1,2,0:T(8,128)S(1)} custom-call(f32[1,64,64]{2,1,0:T(8,128)S(1)} %fusion.23), custom_call_target="InvertDiagBlocksLowerTriangular" | custom-call | tf_op jit(solution)/shard_map/jit(_cho_solve)/triangular_solve | solution.py:18
  176.5 0.7 copy.50
  177.2 17.3 %all-to-all-start.1 = ((s32[1,32,2]{2,0,1:T(1,128)}), s32[1,32,2]{2,0,1:T(1,128)S(1)}, u32[]{:S(2)}, u32[]{:S(2)}) async-start(s32[1,32,2]{2,0,1:T(1,128)} %copy.50), calls=%async_computation.1 | async-start | bytes 32768 | tf_op jit(solution)/shard_map/all_to_all | solution.py:58
  195.0 7.2 %all-to-all-done.1 = s32[1,32,2]{2,0,1:T(1,128)S(1)} async-done(((s32[1,32,2]{2,0,1:T(1,128)}), s32[1,32,2]{2,0,1:T(1,128)S(1)}, u32[]{:S(2)}, u32[]{:S(2)}) %all-to-all-start.1) | async-done | bytes 288 | tf_op jit(solution)/shard_map/all_to_all | solution.py:58
  202.2 1.5 stack.2
  203.7 5.9 %all-to-all-start = ((bf16[32,4,4096]{2,1,0:T(4,128)(2,1)}), bf16[32,4,4096]{2,1,0:T(4,128)(2,1)S(1)}, u32[]{:S(2)}, u32[]{:S(2)}) async-start(bf16[32,4,4096]{2,1,0:T(4,128)(2,1)} %stack.2), calls=%async_computation | async-start | bytes 2097152 | tf_op jit(solution)/shard_map/all_to_all | solution.py:25
  210.9 0.7 reduce.4
  211.8 0.6 reshape.66
  212.5 15.5 %all-to-all-done = bf16[32,4,4096]{2,1,0:T(4,128)(2,1)S(1)} async-done(((bf16[32,4,4096]{2,1,0:T(4,128)(2,1)}), bf16[32,4,4096]{2,1,0:T(4,128)(2,1)S(1)}, u32[]{:S(2)}, u32[]{:S(2)}) %all-to-all-start) | async-done | bytes 1048608 | tf_op jit(solution)/shard_map/all_to_all | solution.py:25
  228.8 23.6 %all-reduce = f32[64,128]{1,0:T(8,128)S(1)} all-reduce(f32[64,128]{1,0:T(8,128)S(1)} %fusion.11), channel_id=2, replica_groups=mesh['dp'=32,'block'=8] {'block'}, use_global_device_ids=true, to_apply=%region_7.10.clone | all-reduce | flops 8192 | bytes 65536
  (38 shorter events, 4.7 us)
Async XLA Ops:
  0.0 12.3 %copy-start = (bf16[1,4096,64]{1,2,0:T(8,128)(2,1)S(1)}, bf16[1,4096,64]{1,2,0:T(8,128)(2,1)}, u32[]{:S(2)}) copy-start(bf16[1,4096,64]{1,2,0:T(8,128)(2,1)} %param.13) | copy-start | bytes 1572868
  0.0 16.3 %copy-start.2 = (bf16[1,4096,64]{1,2,0:T(8,128)(2,1)S(1)}, bf16[1,4096,64]{1,2,0:T(8,128)(2,1)}, u32[]{:S(2)}) copy-start(bf16[1,4096,64]{1,2,0:T(8,128)(2,1)} %param.12) | copy-start | bytes 1572868
  1.4 175.8 %all-to-all-start.2 = ((s32[1,32,1]{2,0,1:T(1,128)}), s32[1,32,1]{2,0,1:T(1,128)S(1)}, u32[]{:S(2)}, u32[]{:S(2)}) async-start(s32[1,32,1]{2,0,1:T(1,128)} %copy.52), calls=%async_computation.2 | async-start | bytes 32768 | tf_op jit(solution)/shard_map/all_to_all | solution.py:59
  12.3 3.9 %copy-start.1 = (bf16[1,512,4096]{2,1,0:T(8,128)(2,1)S(1)}, bf16[1,512,4096]{2,1,0:T(8,128)(2,1)}, u32[]{:S(2)}) copy-start(bf16[1,512,4096]{2,1,0:T(8,128)(2,1)} %param.10) | copy-start | bytes 12582916
  16.1 160.4 %copy-start.4 = (s32[1,32,2]{1,2,0:T(2,128)S(1)}, s32[1,32,2]{1,2,0:T(2,128)}, u32[]{:S(2)}) copy-start(s32[1,32,2]{1,2,0:T(2,128)} %param.15) | copy-start | bytes 772
  16.3 193.3 %copy-start.5 = (u32[256]{0:T(256)S(1)}, u32[256]{0:T(256)}, u32[]{:S(2)}) copy-start(u32[256]{0:T(256)} %constant.72) | copy-start | bytes 3076
  175.8 52.5 %copy-start.3 = (bf16[1,64,4096]{2,1,0:T(8,128)(2,1)S(1)}, bf16[1,64,4096]{2,1,0:T(8,128)(2,1)}, u32[]{:S(2)}) copy-start(bf16[1,64,4096]{2,1,0:T(8,128)(2,1)} %param.14) | copy-start | bytes 1572868
  177.2 25.0 %all-to-all-start.1 = ((s32[1,32,2]{2,0,1:T(1,128)}), s32[1,32,2]{2,0,1:T(1,128)S(1)}, u32[]{:S(2)}, u32[]{:S(2)}) async-start(s32[1,32,2]{2,0,1:T(1,128)} %copy.50), calls=%async_computation.1 | async-start | bytes 32768 | tf_op jit(solution)/shard_map/all_to_all | solution.py:58
  203.7 24.3 %all-to-all-start = ((bf16[32,4,4096]{2,1,0:T(4,128)(2,1)}), bf16[32,4,4096]{2,1,0:T(4,128)(2,1)S(1)}, u32[]{:S(2)}, u32[]{:S(2)}) async-start(bf16[32,4,4096]{2,1,0:T(4,128)(2,1)} %stack.2), calls=%async_computation | async-start | bytes 2097152 | tf_op jit(solution)/shard_map/all_to_all | solution.py:25
